TPU v7x, 256 devices: a whole 4x4x8 slice. The times are simulated.
256 devices in a mesh: dp: 2 (over core), ctx: 32 (over z, y), head: 4 (over x).
Axes of the slice: x: 4, y: 4, z: 8, core: 2. Of those that a mesh axis runs over, the one named last changes fastest.
Arguments:
- queries: bfloat16 [16384, 1536], P(('dp', 'ctx'), 'head'), parts along dimension 0, may hold values from -5 to 5
- keys: bfloat16 [16384, 1536], P(('dp', 'ctx'), 'head'), parts along dimension 0, may hold values from -5 to 5
- values: bfloat16 [16384, 1536], P(('dp', 'ctx'), 'head'), parts along dimension 0, may hold values from -6 to 6
- out_grad: bfloat16 [16384, 1536], P(('dp', 'ctx'), 'head'), parts along dimension 0, may hold values from -6 to 6
- radial_pick: int32 [32, 32], replicated, may hold values from 0 to 15
Outputs:
- attended: bfloat16 [16384, 1536], P(('dp', 'ctx'), 'head'), parts along dimension 0
- query_grad: bfloat16 [16384, 1536], P(('dp', 'ctx'), 'head'), parts along dimension 0
- key_grad: bfloat16 [16384, 1536], P(('dp', 'ctx'), 'head'), parts along dimension 0
- value_grad: bfloat16 [16384, 1536], P(('dp', 'ctx'), 'head'), parts along dimension 0
There are 2 independent parts, one for each index of `dp`. A program takes and returns all parts, laid end to end along the dimension named above; an argument that names none is the same for every part. Nothing has to cross between parts.
All inputs are finite; a program needn't handle non-finite values.
Results may differ from a plain program's by a relative error of at most 0.02.
Values may be sent and summed in bfloat16 or wider, within the bound.
A program may use at most 128 MiB of HBM per device.

v0:
```python
from functools import reduce

import jax
import jax.numpy as jnp
from jax import lax
from jax.sharding import PartitionSpec as P

HD = 128
BLOCK = 64


def padded(array, sides, width):
    for axis, dim in sides:
        size, length = (lax.axis_size(axis), array.shape[dim])
        up = [(i, (i + 1) % size) for i in range(size - 1)]
        down = [(j, i) for i, j in up]
        last = lax.slice_in_dim(array, length - width, length, axis=dim)
        initial = lax.slice_in_dim(array, 0, width, axis=dim)
        before = lax.ppermute(last, axis, up)
        after = lax.ppermute(initial, axis, down)
        array = jnp.concatenate([before, array, after], axis=dim)
    return array


def passed_along(value, axis, steps):
    count = lax.axis_size(axis)
    initial, last = (max(0, -steps), min(count, count - steps))
    return lax.ppermute(value, axis, [(source, source + steps) for source in range(initial, last)])


def live_mask(frame, pick_row, frames, rows):
    blocks = rows // BLOCK
    tile = jnp.arange(rows) // BLOCK
    near_frame = frame - 1 + jnp.arange(3 * rows) // rows
    near_live = (near_frame >= 0) & (near_frame < frames)
    near_mask = jnp.broadcast_to(near_live[None, :], (rows, 3 * rows))
    slot = jnp.arange(frames * BLOCK) // BLOCK
    distance = jnp.abs(frame - slot)
    chosen = jnp.repeat(pick_row, BLOCK) // blocks
    far_mask = (distance[None, :] >= 2) & (
        (distance[None, :] < 4) | (tile[:, None] == chosen[None, :])
    )
    return jnp.concatenate([near_mask, far_mask], axis=1)


def key_groups(near_len, far_len):
    span = max(BLOCK, 2048 // BLOCK * BLOCK)
    groups = [(0, near_len)]
    groups.append((near_len, min(span, far_len)))
    return groups


def per_device(queries, keys, values, out_grad, radial_pick):
    frames = lax.axis_size("ctx")
    frame = lax.axis_index("ctx")
    rows = queries.shape[0]
    width = queries.shape[1]
    blocks = rows // BLOCK
    heads = width // HD
    scale = HD ** (-0.5)
    pair = jnp.stack([keys, values])
    near = padded(pair, (("ctx", 1),), rows)
    column = radial_pick[:, frame]
    sent = pair.reshape(2, blocks, BLOCK, width)[:, column % blocks]
    far = lax.all_to_all(sent, "ctx", split_axis=1, concat_axis=1, tiled=True).reshape(
        2, frames * BLOCK, width
    )
    key_set = jnp.concatenate([near[0], far[0]], 0)
    value_set = jnp.concatenate([near[1], far[1]], 0)
    live = live_mask(frame, radial_pick[frame], frames, rows)
    groups = key_groups(3 * rows, frames * BLOCK)
    out_cols, dq_cols, dk_cols, dv_cols, lse_cols, delta_cols = ([], [], [], [], [], [])
    for head in range(heads):
        low = head * HD
        query_h = queries[:, low : low + HD]
        grad_h = out_grad[:, low : low + HD]

        def scores(begin, size):
            key_part = key_set[begin : begin + size, low : low + HD]
            raw = (
                jnp.einsum("qd,kd->qk", query_h, key_part, preferred_element_type=jnp.float32)
                * scale
            )
            return jnp.where(live[:, begin : begin + size], raw, -jnp.inf)

        tops, totals = ([], [])
        for begin, size in groups:
            masked = scores(begin, size)
            top = jnp.maximum(jnp.max(masked, axis=1, keepdims=True), -1e30)
            tops.append(top)
            totals.append(jnp.sum(jnp.exp(masked - top), axis=1, keepdims=True))
        peak = reduce(jnp.maximum, tops)
        total = reduce(jnp.add, [part * jnp.exp(top - peak) for part, top in zip(totals, tops)])
        lse = peak + jnp.log(total)
        out_acc = jnp.zeros((rows, HD), jnp.float32)
        for begin, size in groups:
            weights = jnp.exp(scores(begin, size) - lse).astype(jnp.bfloat16)
            out_acc = out_acc + jnp.dot(
                weights,
                value_set[begin : begin + size, low : low + HD],
                preferred_element_type=jnp.float32,
            )
        out_h = out_acc.astype(jnp.bfloat16)
        delta = jnp.sum(
            grad_h.astype(jnp.float32) * out_h.astype(jnp.float32), axis=1, keepdims=True
        )
        dq_acc = jnp.zeros((rows, HD), jnp.float32)
        dk_parts, dv_parts = ([], [])
        for begin, size in groups:
            prob = jnp.exp(scores(begin, size) - lse)
            weights = prob.astype(jnp.bfloat16)
            key_part = key_set[begin : begin + size, low : low + HD]
            value_part = value_set[begin : begin + size, low : low + HD]
            dprob = jnp.einsum("qd,kd->qk", grad_h, value_part, preferred_element_type=jnp.float32)
            dscore = (prob * (dprob - delta)).astype(jnp.bfloat16)
            dq_acc = dq_acc + jnp.dot(dscore, key_part, preferred_element_type=jnp.float32) * scale
            dk_parts.append(
                jnp.einsum("qk,qd->kd", dscore, query_h, preferred_element_type=jnp.float32) * scale
            )
            dv_parts.append(
                jnp.einsum("qk,qd->kd", weights, grad_h, preferred_element_type=jnp.float32)
            )
        out_cols.append(out_h)
        dq_cols.append(dq_acc)
        dk_cols.append(jnp.concatenate(dk_parts, 0))
        dv_cols.append(jnp.concatenate(dv_parts, 0))
        lse_cols.append(lse)
        delta_cols.append(delta)
    attended = jnp.concatenate(out_cols, 1)
    query_grad = jnp.concatenate(dq_cols, 1).astype(jnp.bfloat16)
    dk_all = jnp.concatenate(dk_cols, 1)
    dv_all = jnp.concatenate(dv_cols, 1)
    far_part = jnp.stack([dk_all[3 * rows :], dv_all[3 * rows :]]).reshape(2, frames, BLOCK, width)
    back = lax.all_to_all(
        far_part.astype(jnp.bfloat16), "ctx", split_axis=1, concat_axis=1, tiled=True
    ).astype(far_part.dtype)
    onehot = ((column % blocks)[:, None] == jnp.arange(blocks)[None, :]).astype(jnp.float32)
    placed = jnp.einsum("sn,asbw->anbw", onehot, back, precision=lax.Precision.HIGHEST).reshape(
        2, rows, width
    )
    near_grads = jnp.stack([dk_all[: 3 * rows], dv_all[: 3 * rows]])
    from_left = passed_along(near_grads[:, 2 * rows :].astype(jnp.bfloat16), "ctx", 1).astype(
        jnp.float32
    )
    from_right = passed_along(near_grads[:, :rows].astype(jnp.bfloat16), "ctx", -1).astype(
        jnp.float32
    )
    summed = near_grads[:, rows : 2 * rows] + from_left + from_right + placed
    return (attended, query_grad, summed[0].astype(jnp.bfloat16), summed[1].astype(jnp.bfloat16))


def solution(mesh):
    return jax.shard_map(
        per_device,
        mesh=mesh,
        in_specs=(
            P(("dp", "ctx"), "head"),
            P(("dp", "ctx"), "head"),
            P(("dp", "ctx"), "head"),
            P(("dp", "ctx"), "head"),
            P(),
        ),
        out_specs=(
            P(("dp", "ctx"), "head"),
            P(("dp", "ctx"), "head"),
            P(("dp", "ctx"), "head"),
            P(("dp", "ctx"), "head"),
        ),
        check_vma=False,
    )
```

profile of v0, /device:TPU:36, one launch (start us, length us, event | category | flops | bytes accessed | tf_op | source)
XLA Modules:
  0.0 217.3 jit_solution(4365233301840803073)
XLA Ops:
  0.6 1.4 fusion.128
  2.0 1.1 pad_maximum_fusion.4
  3.1 2.6 %gather_fusion = bf16[32,2,64,384]{3,2,1,0:T(8,128)(2,1)} fusion(bf16[2,4,64,384]{3,2,1,0:T(8,128)(2,1)S(1)} %pad_maximum_fusion.4, s32[1024]{0:T(1024)S(1)} %pad_clamp_fusion), kind=kCustom, calls=%fused_computation | custom fusion | bytes 6291584 | tf_op jit(solution)/shard_map/gather | solution.py:64
  5.7 11.5 %all-to-all-start = ((bf16[2,32,64,384]{3,2,0,1:T(8,128)(2,1)}), bf16[2,32,64,384]{3,2,0,1:T(8,128)(2,1)S(1)}, u32[]{:S(2)}, u32[]{:S(2)}) async-start(bf16[2,32,64,384]{3,2,0,1:T(8,128)(2,1)} %bitcast.84), calls=%async_computation | async-start | bytes 6291456 | tf_op jit(solution)/shard_map/all_to_all | solution.py:65
  17.2 1.7 pad_maximum_fusion.3
  19.0 4.6 %collective-permute-start.1 = (bf16[2,256,384]{2,1,0:T(8,128)(2,1)}, bf16[2,256,384]{2,1,0:T(8,128)(2,1)}, u32[]{:S(2)}, u32[]{:S(2)}) collective-permute-start(bf16[2,256,384]{2,1,0:T(8,128)(2,1)} %pad_maximum_fusion.3), channel_id=1, source_target_pairs={{4,0},{8,4},{12,8},{16,12},{20,16},{24,20},{28,24},{32,28},{36,32}... | collective-permute-start | bytes 1179656 | tf_op jit(solution)/shard_map/ppermute | solution.py:20
  23.5 1.9 collective-permute-start
  27.6 1.6 copy.35
  29.2 1.6 copy.36
  30.7 1.6 copy.37
  34.1 58.9 %collective-permute-done.1 = bf16[2,256,384]{2,1,0:T(8,128)(2,1)} collective-permute-done((bf16[2,256,384]{2,1,0:T(8,128)(2,1)}, bf16[2,256,384]{2,1,0:T(8,128)(2,1)}, u32[]{:S(2)}, u32[]{:S(2)}) %collective-permute-start.1) | collective-permute-done | bytes 393248 | tf_op jit(solution)/shard_map/ppermute | solution.py:20
  93.0 3.1 %collective-permute-done = bf16[2,256,384]{2,1,0:T(8,128)(2,1)} collective-permute-done((bf16[2,256,384]{2,1,0:T(8,128)(2,1)}, bf16[2,256,384]{2,1,0:T(8,128)(2,1)}, u32[]{:S(2)}, u32[]{:S(2)}) %collective-permute-start) | collective-permute-done | bytes 393248 | tf_op jit(solution)/shard_map/ppermute | solution.py:19
  96.1 1.3 pad_maximum_fusion.2
  97.4 0.9 slice_bitcast_fusion.2
  106.9 0.9 multiply_reduce_fusion
  109.1 0.9 fusion.155
  111.6 0.9 multiply_reduce_fusion.1
  116.9 0.9 multiply_reduce_fusion.2
  121.3 1.2 maximum_maximum_fusion
  122.7 1.2 maximum_maximum_fusion.1
  124.7 1.8 copy-done.7
  126.6 2.0 pad_maximum_fusion
  128.5 7.6 %all-to-all-start.1 = ((bf16[2,32,64,384]{3,2,0,1:T(8,128)(2,1)}), bf16[2,32,64,384]{3,2,0,1:T(8,128)(2,1)S(1)}, u32[]{:S(2)}, u32[]{:S(2)}) async-start(bf16[2,32,64,384]{3,2,0,1:T(8,128)(2,1)} %pad_maximum_fusion), calls=%async_computation.1 | async-start | bytes 6291456 | tf_op jit(solution)/shard_map/all_to_all | solution.py:134
  137.0 1.3 slice_bitcast_fusion.1
  138.3 1.8 slice_bitcast_fusion
  140.4 1.0 fusion.151
  141.4 3.6 %collective-permute-start.2 = (bf16[2,256,384]{2,1,0:T(8,128)(2,1)}, bf16[2,256,384]{2,1,0:T(8,128)(2,1)}, u32[]{:S(2)}, u32[]{:S(2)}) collective-permute-start(bf16[2,256,384]{2,1,0:T(8,128)(2,1)} %get-tuple-element.20), channel_id=1, source_target_pairs={{0,4},{4,8},{8,12},{12,16},{16,20},{20,24},{24,28},{28,32},{32,36}... | collective-permute-start | bytes 1179656 | tf_op jit(solution)/shard_map/ppermute | solution.py:28
  145.0 4.7 %collective-permute-start.3 = (bf16[2,256,384]{2,1,0:T(8,128)(2,1)}, bf16[2,256,384]{2,1,0:T(8,128)(2,1)}, u32[]{:S(2)}, u32[]{:S(2)}) collective-permute-start(bf16[2,256,384]{2,1,0:T(8,128)(2,1)} %get-tuple-element.21), channel_id=1, source_target_pairs={{4,0},{8,4},{12,8},{16,12},{20,16},{24,20},{28,24},{32,28},{36,32}... | collective-permute-start | bytes 1179656 | tf_op jit(solution)/shard_map/ppermute | solution.py:28
  152.9 56.7 %all-to-all-done.1 = bf16[2,32,64,384]{3,2,0,1:T(8,128)(2,1)S(1)} async-done(((bf16[2,32,64,384]{3,2,0,1:T(8,128)(2,1)}), bf16[2,32,64,384]{3,2,0,1:T(8,128)(2,1)S(1)}, u32[]{:S(2)}, u32[]{:S(2)}) %all-to-all-start.1) | async-done | bytes 3145760 | tf_op jit(solution)/shard_map/all_to_all | solution.py:134
  209.6 1.8 fusion.21
  211.5 3.6 %collective-permute-done.2 = bf16[2,256,384]{2,1,0:T(8,128)(2,1)} collective-permute-done((bf16[2,256,384]{2,1,0:T(8,128)(2,1)}, bf16[2,256,384]{2,1,0:T(8,128)(2,1)}, u32[]{:S(2)}, u32[]{:S(2)}) %collective-permute-start.2) | collective-permute-done | bytes 393248 | tf_op jit(solution)/shard_map/ppermute | solution.py:28
  215.1 1.4 fusion.46
  (167 shorter events, 28.6 us)
Async XLA Ops:
  5.7 11.5 %copy-start.28 = (bf16[256,384]{1,0:T(8,128)(2,1)S(1)}, bf16[256,384]{1,0:T(8,128)(2,1)}, u32[]{:S(2)}) copy-start(bf16[256,384]{1,0:T(8,128)(2,1)} %param.7) | copy-start | bytes 589828
  5.7 21.2 %copy-start.13 = (bf16[256,384]{1,0:T(8,128)(2,1)S(1)}, bf16[256,384]{1,0:T(8,128)(2,1)}, u32[]{:S(2)}) copy-start(bf16[256,384]{1,0:T(8,128)(2,1)} %param.8) | copy-start | bytes 589828
  5.7 97.4 %all-to-all-start = ((bf16[2,32,64,384]{3,2,0,1:T(8,128)(2,1)}), bf16[2,32,64,384]{3,2,0,1:T(8,128)(2,1)S(1)}, u32[]{:S(2)}, u32[]{:S(2)}) async-start(bf16[2,32,64,384]{3,2,0,1:T(8,128)(2,1)} %bitcast.84), calls=%async_computation | async-start | bytes 6291456 | tf_op jit(solution)/shard_map/all_to_all | solution.py:65
  19.0 74.0 %collective-permute-start.1 = (bf16[2,256,384]{2,1,0:T(8,128)(2,1)}, bf16[2,256,384]{2,1,0:T(8,128)(2,1)}, u32[]{:S(2)}, u32[]{:S(2)}) collective-permute-start(bf16[2,256,384]{2,1,0:T(8,128)(2,1)} %pad_maximum_fusion.3), channel_id=1, source_target_pairs={{4,0},{8,4},{12,8},{16,12},{20,16},{24,20},{28,24},{32,28},{36,32}... | collective-permute-start | bytes 1179656 | tf_op jit(solution)/shard_map/ppermute | solution.py:20
  23.5 72.6 %collective-permute-start = (bf16[2,256,384]{2,1,0:T(8,128)(2,1)}, bf16[2,256,384]{2,1,0:T(8,128)(2,1)}, u32[]{:S(2)}, u32[]{:S(2)}) collective-permute-start(bf16[2,256,384]{2,1,0:T(8,128)(2,1)} %pad_maximum_fusion.3), channel_id=1, source_target_pairs={{0,4},{4,8},{8,12},{12,16},{16,20},{20,24},{24,28},{28,32},{32,36}... | collective-permute-start | bytes 1179656 | tf_op jit(solution)/shard_map/ppermute | solution.py:19
  34.1 64.3 %copy-start.31 = (bf16[256,384]{1,0:T(8,128)(2,1)S(1)}, bf16[256,384]{1,0:T(8,128)(2,1)}, u32[]{:S(2)}) copy-start(bf16[256,384]{1,0:T(8,128)(2,1)} %param.5) | copy-start | bytes 589828
  98.4 3.7 %copy-start.26 = (bf16[768,384]{1,0:T(8,128)(2,1)}, bf16[768,384]{1,0:T(8,128)(2,1)S(1)}, u32[]{:S(2)}) copy-start(bf16[768,384]{1,0:T(8,128)(2,1)S(1)} %get-tuple-element.23) | copy-start | bytes 1769476
  98.7 3.9 %copy-start.44 = (f32[256]{0:T(256)}, f32[256]{0:T(256)S(1)}, u32[]{:S(2)}) copy-start(f32[256]{0:T(256)S(1)} %get-tuple-element.31) | copy-start | bytes 3076
  103.6 10.2 %copy-start.29 = (bf16[1,32,64,384]{3,2,0,1:T(8,128)(2,1)}, bf16[1,32,64,384]{3,2,0,1:T(8,128)(2,1)S(1)}, u32[]{:S(2)}) copy-start(bf16[1,32,64,384]{3,2,0,1:T(8,128)(2,1)S(1)} %get-tuple-element.18) | copy-start | bytes 4718596
  108.1 10.8 %copy-start.20 = (bf16[768,256]{1,0:T(8,128)(2,1)}, bf16[768,256]{1,0:T(8,128)(2,1)S(1)}, u32[]{:S(2)}) copy-start(bf16[768,256]{1,0:T(8,128)(2,1)S(1)} %fusion.32) | copy-start | bytes 1179652
  108.7 10.5 %copy-start.14 = (bf16[256,2048]{0,1:T(8,128)(2,1)}, bf16[256,2048]{0,1:T(8,128)(2,1)S(1)}, u32[]{:S(2)}) copy-start(bf16[256,2048]{0,1:T(8,128)(2,1)S(1)} %fusion.16) | copy-start | bytes 3145732
  112.8 7.1 %copy-start.22 = (bf16[768,256]{1,0:T(8,128)(2,1)}, bf16[768,256]{1,0:T(8,128)(2,1)S(1)}, u32[]{:S(2)}) copy-start(bf16[768,256]{1,0:T(8,128)(2,1)S(1)} %fusion.31) | copy-start | bytes 1179652
  113.3 6.8 %copy-start.16 = (bf16[256,2048]{0,1:T(8,128)(2,1)}, bf16[256,2048]{0,1:T(8,128)(2,1)S(1)}, u32[]{:S(2)}) copy-start(bf16[256,2048]{0,1:T(8,128)(2,1)S(1)} %fusion.15) | copy-start | bytes 3145732
  118.4 2.5 %copy-start.18 = (bf16[256,2048]{0,1:T(8,128)(2,1)}, bf16[256,2048]{0,1:T(8,128)(2,1)S(1)}, u32[]{:S(2)}) copy-start(bf16[256,2048]{0,1:T(8,128)(2,1)S(1)} %fusion.14) | copy-start | bytes 3145732
  122.5 2.1 copy-start.6
  124.5 2.0 copy-start.7
  128.5 7.6 %copy-start.36 = (bf16[256,128]{0,1:T(8,128)(2,1)S(1)}, bf16[256,128]{0,1:T(8,128)(2,1)}, u32[]{:S(2)}) copy-start(bf16[256,128]{0,1:T(8,128)(2,1)} %get-tuple-element.42) | copy-start | bytes 196612
  128.5 7.6 %copy-start.37 = (bf16[256,128]{0,1:T(8,128)(2,1)S(1)}, bf16[256,128]{0,1:T(8,128)(2,1)}, u32[]{:S(2)}) copy-start(bf16[256,128]{0,1:T(8,128)(2,1)} %get-tuple-element.44) | copy-start | bytes 196612
  128.5 7.6 %copy-start.38 = (bf16[256,128]{0,1:T(8,128)(2,1)S(1)}, bf16[256,128]{0,1:T(8,128)(2,1)}, u32[]{:S(2)}) copy-start(bf16[256,128]{0,1:T(8,128)(2,1)} %get-tuple-element.46) | copy-start | bytes 196612
  128.5 81.0 %all-to-all-start.1 = ((bf16[2,32,64,384]{3,2,0,1:T(8,128)(2,1)}), bf16[2,32,64,384]{3,2,0,1:T(8,128)(2,1)S(1)}, u32[]{:S(2)}, u32[]{:S(2)}) async-start(bf16[2,32,64,384]{3,2,0,1:T(8,128)(2,1)} %pad_maximum_fusion), calls=%async_computation.1 | async-start | bytes 6291456 | tf_op jit(solution)/shard_map/all_to_all | solution.py:134
  138.3 2.0 copy-start.8
  140.1 9.6 %copy-start.15 = (bf16[256,2048]{0,1:T(8,128)(2,1)S(1)}, bf16[256,2048]{0,1:T(8,128)(2,1)}, u32[]{:S(2)}) copy-start(bf16[256,2048]{0,1:T(8,128)(2,1)} %copy-done.14) | copy-start | bytes 3145732
  140.1 9.6 %copy-start.30 = (bf16[1,32,64,384]{3,2,0,1:T(8,128)(2,1)S(1)}, bf16[1,32,64,384]{3,2,0,1:T(8,128)(2,1)}, u32[]{:S(2)}) copy-start(bf16[1,32,64,384]{3,2,0,1:T(8,128)(2,1)} %copy-done.29) | copy-start | bytes 4718596
  140.3 9.8 %copy-start.21 = (bf16[768,256]{1,0:T(8,128)(2,1)S(1)}, bf16[768,256]{1,0:T(8,128)(2,1)}, u32[]{:S(2)}) copy-start(bf16[768,256]{1,0:T(8,128)(2,1)} %copy-done.20) | copy-start | bytes 1179652
  140.4 9.8 %copy-start.27 = (bf16[768,384]{1,0:T(8,128)(2,1)S(1)}, bf16[768,384]{1,0:T(8,128)(2,1)}, u32[]{:S(2)}) copy-start(bf16[768,384]{1,0:T(8,128)(2,1)} %copy-done.26) | copy-start | bytes 1769476
  140.4 10.1 %copy-start.17 = (bf16[256,2048]{0,1:T(8,128)(2,1)S(1)}, bf16[256,2048]{0,1:T(8,128)(2,1)}, u32[]{:S(2)}) copy-start(bf16[256,2048]{0,1:T(8,128)(2,1)} %copy-done.16) | copy-start | bytes 3145732
  141.4 73.7 %collective-permute-start.2 = (bf16[2,256,384]{2,1,0:T(8,128)(2,1)}, bf16[2,256,384]{2,1,0:T(8,128)(2,1)}, u32[]{:S(2)}, u32[]{:S(2)}) collective-permute-start(bf16[2,256,384]{2,1,0:T(8,128)(2,1)} %get-tuple-element.20), channel_id=1, source_target_pairs={{0,4},{4,8},{8,12},{12,16},{16,20},{20,24},{24,28},{28,32},{32,36}... | collective-permute-start | bytes 1179656 | tf_op jit(solution)/shard_map/ppermute | solution.py:28
  145.0 5.8 %copy-start.23 = (bf16[768,256]{1,0:T(8,128)(2,1)S(1)}, bf16[768,256]{1,0:T(8,128)(2,1)}, u32[]{:S(2)}) copy-start(bf16[768,256]{1,0:T(8,128)(2,1)} %copy-done.22) | copy-start | bytes 1179652
  145.0 70.1 %collective-permute-start.3 = (bf16[2,256,384]{2,1,0:T(8,128)(2,1)}, bf16[2,256,384]{2,1,0:T(8,128)(2,1)}, u32[]{:S(2)}, u32[]{:S(2)}) collective-permute-start(bf16[2,256,384]{2,1,0:T(8,128)(2,1)} %get-tuple-element.21), channel_id=1, source_target_pairs={{4,0},{8,4},{12,8},{16,12},{20,16},{24,20},{28,24},{32,28},{36,32}... | collective-permute-start | bytes 1179656 | tf_op jit(solution)/shard_map/ppermute | solution.py:28
  150.8 58.7 %copy-start.46 = (s32[32]{0:T(128)S(1)}, s32[32]{0:T(128)}, u32[]{:S(2)}) copy-start(s32[32]{0:T(128)} %get-tuple-element.16) | copy-start | bytes 388
  209.6 5.5 %copy-start.9 = (f32[1,768,384]{2,1,0:T(8,128)S(1)}, f32[1,768,384]{2,1,0:T(8,128)}, u32[]{:S(2)}) copy-start(f32[1,768,384]{2,1,0:T(8,128)} %copy-done.8) | copy-start | bytes 3538948
  209.6 5.5 %copy-start.11 = (f32[1,768,384]{2,1,0:T(8,128)S(1)}, f32[1,768,384]{2,1,0:T(8,128)}, u32[]{:S(2)}) copy-start(f32[1,768,384]{2,1,0:T(8,128)} %copy-done.10) | copy-start | bytes 3538948
  (24 other events, 24.5 us)
where the time goes:
time: 218 us; the launch traced here: 217 us
  waiting for transfers between devices  122 us (56%)
  starting transfers between devices  33.9 us (16%)
  local copies, waits for them, and re-layouts  25.7 us (12%)
  matrix products  18.3 us (8%)
  other arithmetic  15.5 us (7%)
    ppermute x1, waiting for transfers between devices, padded(): after = lax.ppermute(initial, axis, down)  58.9 us
    all_to_all x1, waiting for transfers between devices, per_device(): lax.all_to_all(far_part.astype(jnp.bfloat16), 'ctx', split_axis=1, concat...  56.7 us
    unnamed x106, local copies, waits for them, and re-layouts  15 us
    all_to_all x1, starting transfers between devices, per_device(): lax.all_to_all(sent, 'ctx', split_axis=1, concat_axis=1, tiled=True)  11.5 us
    ppermute x2, starting transfers between devices, passed_along(): lax.ppermute(value, axis, [(source, source + steps) for source in range(i...  8.34 us
    all_to_all x1, starting transfers between devices, per_device(): lax.all_to_all(far_part.astype(jnp.bfloat16), 'ctx', split_axis=1, concat...  7.55 us
    ppermute x1, starting transfers between devices, padded(): after = lax.ppermute(initial, axis, down)  4.57 us
  transfers between devices with their start and end apart: 6, of which 4 were waited for; matrix products, arithmetic and copies ran while one was open for 11% of the time, Pallas kernels for 0%

commit v1 on v0

v1 whole, which is shorter than its diff:
```python
import functools

import jax
import jax.numpy as jnp
from jax import lax
from jax.experimental import pallas as pl
from jax.experimental.pallas import tpu as pltpu
from jax.sharding import PartitionSpec as P

HD = 128
BLOCK = 64
NZ = 8
NY = 4
FT = 256
NEG = -1e30
FLOOR = -1e20
MESH = pl.DeviceIdType.MESH

NEAR, FAR0, FAR1, FAR2, FAR3, KEYS = 0, 256, 448, 576, 704, 768

NT = (((1,), (1,)), ((), ()))
NN = (((1,), (0,)), ((), ()))
TN = (((0,), (0,)), ((), ()))


def mm(a, b, dims):
    return lax.dot_general(a, b, dims, preferred_element_type=jnp.float32)


def kernel(
    pick_ref, q_ref, k_ref, v_ref, do_ref,
    out_ref, dq_ref, dk_ref, dv_ref,
    q_all, do_all, do_t, k_a, v_a, k_b, v_b, k_c, v_c, k_d, v_d,
    k_sel, v_sel, sc, st, fin, o_t, dq_t, o_send, o_recv, dq_send, dq_recv, acc, rs_send, rs_recv,
    z_ssem, z_rsem, y_ssem, y_rsem, r_ssem, r_rsem,
):
    width = q_ref.shape[1]
    heads = width // HD
    scale = HD ** -0.5
    me = lax.axis_index("ctx")
    z, y = me // NY, me % NY

    def at(dz, dy):
        return {"ctx": ((z + dz + NZ) % NZ) * NY + (y + dy) % NY}

    def cols(h):
        return slice(h * HD, (h + 1) * HD)

    barrier = pltpu.get_barrier_semaphore()
    for peer in (at(1, 0), at(-1, 0), at(0, 1), at(0, 2), at(0, 3)):
        pl.semaphore_signal(barrier, inc=1, device_id=peer, device_id_type=MESH)
    pl.semaphore_wait(barrier, 5)

    key_slot = {0: k_a.at[0], 1: k_a.at[1], -1: k_a.at[2], 2: k_b.at[0], -2: k_b.at[1],
                3: k_c.at[0], -3: k_c.at[1], 4: k_d.at[0], -4: k_d.at[0]}
    val_slot = {0: v_a.at[0], 1: v_a.at[1], -1: v_a.at[2], 2: v_b.at[0], -2: v_b.at[1],
                3: v_c.at[0], -3: v_c.at[1], 4: v_d.at[0], -4: v_d.at[0]}

    def z_copy(way, step, kind):
        sign = -1 if way == 0 else 1
        slots = (key_slot, val_slot)[kind]
        src = (k_ref, v_ref)[kind] if step == 1 else slots[sign * (step - 1)]
        return pltpu.make_async_remote_copy(
            src_ref=src,
            dst_ref=slots[sign * step],
            send_sem=z_ssem.at[way, step - 1, kind],
            recv_sem=z_rsem.at[way, step - 1, kind],
            device_id=at(-sign, 0),
            device_id_type=MESH,
        )

    def y_copy(src, dst, what, t):
        return pltpu.make_async_remote_copy(
            src_ref=src,
            dst_ref=dst,
            send_sem=y_ssem.at[what, t - 1],
            recv_sem=y_rsem.at[what, 3 - t],
            device_id=at(0, t),
            device_id_type=MESH,
        )

    sent = []

    def start(copy):
        copy.start()
        sent.append(copy)

    gather = {(w, s, k): z_copy(w, s, k) for w in (0, 1) for s in (1, 2, 3, 4) for k in (0, 1)}
    for kind in (0, 1):
        for way in (0, 1):
            start(gather[way, 1, kind])
    q_copies = [y_copy(q_ref, q_all.at[4 - t], 0, t) for t in (1, 3, 2)]
    do_copies = [y_copy(do_ref, do_all.at[4 - t], 1, t) for t in (1, 3, 2)]
    for copy in q_copies + do_copies:
        start(copy)

    k_a[0] = k_ref[...]
    v_a[0] = v_ref[...]
    q_all[0] = q_ref[...]
    do_all[0] = do_ref[...]

    @pl.loop(0, NY)
    def _(i):
        st[0, i, 0:heads] = jnp.full((heads, FT), FLOOR, jnp.float32)
        st[0, i, heads : 3 * heads] = jnp.zeros((2 * heads, FT), jnp.float32)
        o_t[i] = jnp.zeros((width, FT), jnp.float32)
        dq_t[i] = jnp.zeros((width, FT), jnp.float32)

    @pl.loop(0, NZ)
    def _(i):
        for kind in (0, 1):
            acc[i, kind] = jnp.zeros((FT, width), jnp.float32)

    tile = lax.broadcasted_iota(jnp.int32, (1, FT), 1) // BLOCK

    group0 = ((0, k_a, v_a, 0), (1, k_a, v_a, 1), (-1, k_a, v_a, 2))
    group1 = ((2, k_b, v_b, 0), (-2, k_b, v_b, 1))
    group2 = ((3, k_c, v_c, 0), (-3, k_c, v_c, 1))
    group3 = ((4, k_d, v_d, 0),)

    def chosen(qi, r):
        a = z * NY + (y + qi) % NY
        b = ((z + r + NZ) % NZ) * NY + y
        return pick_ref[a, b], jnp.abs(a - b)

    def bias_row(qi, r):
        pick, dist = chosen(qi, r)
        want = jnp.broadcast_to(pick, (1, FT)) >> 2
        row = jnp.where(tile == want, 0.0, NEG).astype(jnp.float32)
        row = jnp.maximum(row, jnp.where(dist < 4, 0.0, NEG).astype(jnp.float32))
        return jnp.minimum(row, jnp.where(dist < 2, NEG, 0.0).astype(jnp.float32))

    def select(group, begin):
        begin -= FAR0

        @pl.loop(0, NY)
        def _(qi):
            for g, (r, k, v, i) in enumerate(group):
                pick, _ = chosen(qi, r)
                place = jnp.broadcast_to(pick, (1, width)) & 3
                hits = [jnp.where(place == n, 1.0, 0.0).astype(k.dtype) for n in range(4)]
                to = slice(begin + g * BLOCK, begin + (g + 1) * BLOCK)
                for ref, dst in ((k, k_sel), (v, v_sel)):
                    parts = [ref[i, n * BLOCK : (n + 1) * BLOCK] * hits[n] for n in range(4)]
                    dst[qi, to] = (parts[0] + parts[1]) + (parts[2] + parts[3])

    def rows(parts):
        return parts[0] if len(parts) == 1 else jnp.concatenate(parts, 0)

    def update(qi, h, s, values):
        m_old = st[0, qi, h : h + 1]
        l_old = st[0, qi, heads + h : heads + h + 1]
        m_new = jnp.maximum(m_old, jnp.max(s, axis=0, keepdims=True))
        p = jnp.exp(s - m_new)
        alpha = jnp.exp(m_old - m_new)
        st[0, qi, h : h + 1] = m_new
        st[0, qi, heads + h : heads + h + 1] = l_old * alpha + jnp.sum(p, axis=0, keepdims=True)
        o_t[qi, cols(h)] = o_t[qi, cols(h)] * alpha + mm(values, p.astype(jnp.bfloat16), TN)

    def forward_far(group, begin):
        size = BLOCK * len(group)
        select(group, begin)

        @pl.loop(0, NY)
        def _(qi):
            bias = [bias_row(qi, r) for r, _, _, _ in group]
            bias = rows([jnp.broadcast_to(row, (BLOCK, FT)) for row in bias])
            for h in range(heads):
                ks = k_sel[qi, begin - FAR0 : begin - FAR0 + size, cols(h)]
                vs = v_sel[qi, begin - FAR0 : begin - FAR0 + size, cols(h)]
                s = mm(ks, q_all[qi, :, cols(h)], NT) * scale + bias
                sc[qi, h, begin : begin + size] = s
                update(qi, h, s, vs)

    def near_place(i):
        qi = jnp.where(i == 2, 3, i)
        over = ((i == 1) & (y == NY - 1)) | ((i == 2) & (y == 0))
        slot = jnp.where(over, jnp.where(i == 1, 2, 1), 0)
        r = jnp.where(over, jnp.where(i == 1, NZ - 1, 1), 0)
        dead = ((i == 1) & (y == NY - 1) & (z == 0)) | ((i == 2) & (y == 0) & (z == NZ - 1))
        return qi, slot, r, jnp.where(dead, NEG, 0.0).astype(jnp.float32)

    def forward_near():
        @pl.loop(0, 3)
        def _(i):
            qi, slot, _, bias = near_place(i)
            for h in range(heads):
                s = mm(k_a[slot, :, cols(h)], q_all[qi, :, cols(h)], NT) * scale + bias
                sc[qi, h, NEAR : NEAR + FT] = s
                update(qi, h, s, v_a[slot, :, cols(h)])

    def back(qi, h, begin, size, ks, vs):
        p = jnp.exp(sc[qi, h, begin : begin + size] - fin[qi, h : h + 1])
        grad = do_all[qi, :, cols(h)]
        dp = mm(vs, grad, NT)
        ds = (p * (dp - fin[qi, heads + h : heads + h + 1])).astype(jnp.bfloat16)
        dk = mm(ds, q_all[qi, :, cols(h)], NN) * scale
        dv = mm(p.astype(jnp.bfloat16), grad, NN)
        dq_t[qi, cols(h)] = dq_t[qi, cols(h)] + mm(ks, ds, TN)
        return dk, dv

    def backward_far(group, begin):
        size = BLOCK * len(group)

        @pl.loop(0, NY)
        def _(qi):
            for h in range(heads):
                ks = k_sel[qi, begin - FAR0 : begin - FAR0 + size, cols(h)]
                vs = v_sel[qi, begin - FAR0 : begin - FAR0 + size, cols(h)]
                parts = back(qi, h, begin, size, ks, vs)
                for g, (r, _, _, _) in enumerate(group):
                    pick, _ = chosen(qi, r)
                    place = jnp.broadcast_to(pick, (1, HD)) & 3
                    for n in range(FT // BLOCK):
                        hit = jnp.where(place == n, 1.0, 0.0).astype(jnp.float32)
                        where = slice(n * BLOCK, (n + 1) * BLOCK)
                        for kind in (0, 1):
                            part = parts[kind][g * BLOCK : (g + 1) * BLOCK]
                            acc[r % NZ, kind, where, cols(h)] += part * hit

    def backward_near():
        @pl.loop(0, 3)
        def _(i):
            qi, slot, r, _ = near_place(i)
            for h in range(heads):
                parts = back(qi, h, NEAR, FT, k_a[slot, :, cols(h)], v_a[slot, :, cols(h)])
                for kind in (0, 1):
                    acc[r, kind, :, cols(h)] += parts[kind]

    for kind in (0, 1):
        for way in (0, 1):
            gather[way, 1, kind].wait_recv()
            start(gather[way, 2, kind])
    for copy in q_copies:
        copy.wait_recv()
    forward_near()
    forward_far(group0, FAR0)
    for kind in (0, 1):
        for way in (0, 1):
            gather[way, 2, kind].wait_recv()
            start(gather[way, 3, kind])
    forward_far(group1, FAR1)
    for kind in (0, 1):
        for way in (0, 1):
            gather[way, 3, kind].wait_recv()
            if way == kind:
                start(gather[way, 4, kind])
    forward_far(group2, FAR2)
    for copy in do_copies:
        copy.wait_recv()

    @pl.loop(0, NY)
    def _(i):
        for h in range(heads):
            do_t[i, cols(h)] = do_all[i, :, cols(h)].astype(jnp.float32).T

    gather[0, 4, 0].wait_recv()
    gather[1, 4, 1].wait_recv()
    forward_far(group3, FAR3)

    @pl.loop(0, NY)
    def _(i):
        for h in range(heads):
            st[0, i, 2 * heads + h : 2 * heads + h + 1] = jnp.sum(
                o_t[i, cols(h)] * do_t[i, cols(h)], axis=0, keepdims=True
            )

    st_copies = [y_copy(st.at[0], st.at[4 - t], 2, t) for t in (2, 1, 3)]
    for copy in st_copies:
        start(copy)
    for copy in st_copies:
        copy.wait_recv()
    for qi in range(NY):
        peer = [st[s, (qi - s) % NY] for s in range(NY)]
        top = functools.reduce(jnp.maximum, [x[0:heads] for x in peer])
        gain = [jnp.exp(x[0:heads] - top) for x in peer]
        total = functools.reduce(jnp.add, [x[heads : 2 * heads] * g for x, g in zip(peer, gain)])
        delta = functools.reduce(
            jnp.add, [x[2 * heads : 3 * heads] * g for x, g in zip(peer, gain)]
        )
        fin[qi, 0:heads] = top + jnp.log(total)
        fin[qi, heads : 2 * heads] = delta / total
        fin[qi, 2 * heads : 3 * heads] = gain[0] / total

    def r_copy(way, step, kind):
        return pltpu.make_async_remote_copy(
            src_ref=rs_send.at[way, step, kind],
            dst_ref=rs_recv.at[way, step, kind],
            send_sem=r_ssem.at[way, step, kind],
            recv_sem=r_rsem.at[way, step, kind],
            device_id=at(1 if way == 0 else -1, 0),
            device_id_type=MESH,
        )

    scatter = {(w, s, k): r_copy(w, s, k) for w in (0, 1) for s in range(4) for k in (0, 1)}

    def pass_on(step, way, kind):
        r = (4 - step) if way == 0 else (step - 4) % NZ
        part = acc[r, kind]
        if step >= 2 or (step == 1 and way == kind):
            scatter[way, step - 1, kind].wait_recv()
            part = part + rs_recv[way, step - 1, kind].astype(jnp.float32)
        rs_send[way, step, kind] = part.astype(jnp.bfloat16)
        start(scatter[way, step, kind])

    backward_far(group3, FAR3)
    pass_on(0, 0, 0)
    pass_on(0, 1, 1)
    backward_far(group2, FAR2)
    for kind in (0, 1):
        for way in (0, 1):
            pass_on(1, way, 1 - kind if way == 0 else kind)

    o_copies = []
    for t in (2, 1, 3):
        for h in range(heads):
            weight = fin[t, 2 * heads + h : 2 * heads + h + 1]
            o_send[t - 1, cols(h)] = (o_t[t, cols(h)] * weight).astype(jnp.bfloat16)
        o_copies.append(y_copy(o_send.at[t - 1], o_recv.at[3 - t], 3, t))
        start(o_copies[-1])

    backward_far(group1, FAR1)
    for kind in (0, 1):
        for way in (0, 1):
            pass_on(2, way, kind)
    backward_near()
    backward_far(group0, FAR0)
    dq_copies = []
    for t in (2, 1, 3):
        dq_send[t - 1] = (dq_t[t] * scale).astype(jnp.bfloat16)
        dq_copies.append(y_copy(dq_send.at[t - 1], dq_recv.at[3 - t], 4, t))
        start(dq_copies[-1])
    for kind in (0, 1):
        for way in (0, 1):
            pass_on(3, way, kind)

    for copy in o_copies:
        copy.wait_recv()
    for h in range(heads):
        total = o_t[0, cols(h)] * fin[0, 2 * heads + h : 2 * heads + h + 1]
        for i in range(3):
            total = total + o_recv[i, cols(h)].astype(jnp.float32)
        out_ref[:, cols(h)] = total.T.astype(jnp.bfloat16)
    for copy in dq_copies:
        copy.wait_recv()
    for h in range(heads):
        total = dq_t[0, cols(h)] * scale
        for i in range(3):
            total = total + dq_recv[i, cols(h)].astype(jnp.float32)
        dq_ref[:, cols(h)] = total.T.astype(jnp.bfloat16)
    for kind, ref in ((0, dk_ref), (1, dv_ref)):
        total = acc[0, kind]
        for way in (0, 1):
            scatter[way, 3, kind].wait_recv()
            total = total + rs_recv[way, 3, kind].astype(jnp.float32)
        ref[...] = total.astype(jnp.bfloat16)
    for copy in sent:
        copy.wait_send()


def per_device(queries, keys, values, out_grad, radial_pick):
    width = queries.shape[1]
    heads = width // HD
    bf, f32 = jnp.bfloat16, jnp.float32
    vmem = pl.BlockSpec(memory_space=pltpu.VMEM)
    shape = jax.ShapeDtypeStruct((FT, width), bf)
    dma = pltpu.SemaphoreType.DMA
    return pl.pallas_call(
        kernel,
        out_shape=(shape,) * 4,
        in_specs=[pl.BlockSpec(memory_space=pltpu.SMEM)] + [vmem] * 4,
        out_specs=(vmem,) * 4,
        scratch_shapes=[
            pltpu.VMEM((NY, FT, width), bf),
            pltpu.VMEM((NY, FT, width), bf),
            pltpu.VMEM((NY, width, FT), f32),
            pltpu.VMEM((3, FT, width), bf),
            pltpu.VMEM((3, FT, width), bf),
            pltpu.VMEM((2, FT, width), bf),
            pltpu.VMEM((2, FT, width), bf),
            pltpu.VMEM((2, FT, width), bf),
            pltpu.VMEM((2, FT, width), bf),
            pltpu.VMEM((1, FT, width), bf),
            pltpu.VMEM((1, FT, width), bf),
            pltpu.VMEM((NY, KEYS - FAR0, width), bf),
            pltpu.VMEM((NY, KEYS - FAR0, width), bf),
            pltpu.VMEM((NY, heads, KEYS, FT), f32),
            pltpu.VMEM((NY, NY, 3 * heads, FT), f32),
            pltpu.VMEM((NY, 3 * heads, FT), f32),
            pltpu.VMEM((NY, width, FT), f32),
            pltpu.VMEM((NY, width, FT), f32),
            pltpu.VMEM((3, width, FT), bf),
            pltpu.VMEM((3, width, FT), bf),
            pltpu.VMEM((3, width, FT), bf),
            pltpu.VMEM((3, width, FT), bf),
            pltpu.VMEM((NZ, 2, FT, width), f32),
            pltpu.VMEM((2, 4, 2, FT, width), bf),
            pltpu.VMEM((2, 4, 2, FT, width), bf),
            dma((2, 4, 2)),
            dma((2, 4, 2)),
            dma((5, 3)),
            dma((5, 3)),
            dma((2, 4, 2)),
            dma((2, 4, 2)),
        ],
        compiler_params=pltpu.CompilerParams(
            collective_id=0, has_side_effects=True, vmem_limit_bytes=60 * 1024 * 1024
        ),
        name="radial_attention",
    )(radial_pick, queries, keys, values, out_grad)


def solution(mesh):
    spec = P(("dp", "ctx"), "head")
    return jax.shard_map(
        per_device,
        mesh=mesh,
        in_specs=(spec, spec, spec, spec, P()),
        out_specs=(spec,) * 4,
        check_vma=False,
    )
```

time: 218 us -> 86.9 us (0.40)
  waiting for transfers between devices: 122 us -> 0 us
  Pallas kernels: 0 us -> 80.7 us
  starting transfers between devices: 33.9 us -> 0 us
  local copies, waits for them, and re-layouts: 25.7 us -> 4.34 us
  matrix products: 18.3 us -> 0 us
  other arithmetic: 15.5 us -> 0 us
    pallas_call x0 -> x1, Pallas kernels: none -> 80.7 us  [per_device(): pl.pallas_call(kernel, out_shape=(shape,) * 4, in_specs=[pl.BlockSpec(mem...]
    ppermute x4 -> x0, waiting for transfers between devices: 65.6 us -> none  [the longest x1 58.9 us: padded(): after = lax.ppermute(initial, axis, down)]
    all_to_all x2 -> x0, waiting for transfers between devices: 56.7 us -> none  [the longest x1 56.7 us: per_device(): lax.all_to_all(far_part.astype(jnp.bfloat16), 'ctx', split_axis=1, concat...]
    all_to_all x2 -> x0, starting transfers between devices: 19 us -> none  [the longest x1 11.5 us: per_device(): lax.all_to_all(sent, 'ctx', split_axis=1, concat_axis=1, tiled=True)]
    dot_general x37 -> x0, matrix products: 18.3 us -> none  [the longest x6 4.22 us: per_device(): jnp.dot(weights, value_set[begin:begin + size, low:low + HD], preferred_e...]
    ppermute x4 -> x0, starting transfers between devices: 14.8 us -> none  [the longest x2 8.34 us: passed_along(): lax.ppermute(value, axis, [(source, source + steps) for source in range(i...]
    unnamed x106 -> x10, local copies, waits for them, and re-layouts: 15 us -> 4.34 us
    another operation x5 -> x0, other arithmetic: 6.31 us -> none  [the longest x2 2.78 us: per_device(): pair = jnp.stack([keys, values])]
  transfers between devices with their start and end apart: 6 -> 0, of which waited for: 4 -> 0; matrix products, arithmetic and copies ran while one was open for 11% -> 0% of each run, Pallas kernels for 0% -> 0%
where the time goes in v1:
time: 86.9 us; the launch traced here: 85.7 us
  Pallas kernels  80.7 us (93%)
  local copies, waits for them, and re-layouts  4.34 us (5%)
    pallas_call x1, Pallas kernels, per_device(): pl.pallas_call(kernel, out_shape=(shape,) * 4, in_specs=[pl.BlockSpec(mem...  80.7 us
    unnamed x10, local copies, waits for them, and re-layouts  4.34 us

profile of v1, /device:TPU:36, one launch (start us, length us, event | category | flops | bytes accessed | tf_op | source)
XLA Modules:
  0.0 85.7 jit_solution(13170814742466445102)
XLA Ops:
  0.6 80.7 %radial_attention.1 = (bf16[256,384]{1,0:T(8,128)(2,1)}, bf16[256,384]{1,0:T(8,128)(2,1)}, bf16[256,384]{1,0:T(8,128)(2,1)}, bf16[256,384]{1,0:T(8,128)(2,1)}) custom-call(s32[32,32]{1,0:T(8,128)} %pick_ref.1, bf16[256,384]{1,0:T(8,128)(2,1)} %q_ref.1, bf16[256,384]{1,0:T(8,128)(2,1)} %k_ref.1, bf16[256,384]{1,0:T(8,128)(2,1)} %v_ref.1, bf16[256,384]{1,0:T(8,128)(2,1)} %do_ref.1), custom_call_target="tpu_custom_call" | custom-call | tf_op jit(solution)/shard_map/radial_attention/pallas_call | solution.py:368
  81.3 0.0 copy-start.2
  81.3 1.7 %copy.13 = bf16[256,384]{1,0:T(8,128)(2,1)} copy(bf16[256,384]{1,0:T(8,128)(2,1)} %get-tuple-element.8) | data formatting | bytes 393216
  83.0 0.0 copy-done.2
  83.0 0.0 copy-start.1
  83.0 0.7 copy.14
  83.7 0.3 copy-done.1
  84.0 0.0 copy-start
  84.0 0.7 copy.15
  84.7 0.3 copy-done
  85.0 0.7 copy.16
Async XLA Ops:
  81.3 1.7 %copy-start.2 = (bf16[256,384]{1,0:T(8,128)(2,1)S(1)}, bf16[256,384]{1,0:T(8,128)(2,1)}, u32[]{:S(2)}) copy-start(bf16[256,384]{1,0:T(8,128)(2,1)} %get-tuple-element.9) | copy-start | bytes 589828
  83.0 1.0 %copy-start.1 = (bf16[256,384]{1,0:T(8,128)(2,1)S(1)}, bf16[256,384]{1,0:T(8,128)(2,1)}, u32[]{:S(2)}) copy-start(bf16[256,384]{1,0:T(8,128)(2,1)} %get-tuple-element.10) | copy-start | bytes 589828
  84.0 1.0 %copy-start = (bf16[256,384]{1,0:T(8,128)(2,1)S(1)}, bf16[256,384]{1,0:T(8,128)(2,1)}, u32[]{:S(2)}) copy-start(bf16[256,384]{1,0:T(8,128)(2,1)} %get-tuple-element.11) | copy-start | bytes 589828

commit v2 on v1

--- a/solution.py
+++ b/solution.py
@@ -32,7 +32,7 @@
     out_ref, dq_ref, dk_ref, dv_ref,
     q_all, do_all, do_t, k_a, v_a, k_b, v_b, k_c, v_c, k_d, v_d,
     k_sel, v_sel, sc, st, fin, o_t, dq_t, o_send, o_recv, dq_send, dq_recv, acc, rs_send, rs_recv,
-    z_ssem, z_rsem, y_ssem, y_rsem, r_ssem, r_rsem,
+    z_ssem, z_rsem, y_ssem, y_rsem, r_ssem, r_rsem, l_sem,
 ):
     width = q_ref.shape[1]
     heads = width // HD
@@ -46,6 +46,12 @@
     def cols(h):
         return slice(h * HD, (h + 1) * HD)
 
+    own = [
+        pltpu.make_async_copy(src, dst.at[0], l_sem.at[i])
+        for i, (src, dst) in enumerate(((k_ref, k_a), (v_ref, v_a), (q_ref, q_all), (do_ref, do_all)))
+    ]
+    for copy in own:
+        copy.start()
     barrier = pltpu.get_barrier_semaphore()
     for peer in (at(1, 0), at(-1, 0), at(0, 1), at(0, 2), at(0, 3)):
         pl.semaphore_signal(barrier, inc=1, device_id=peer, device_id_type=MESH)
@@ -85,7 +91,10 @@
         copy.start()
         sent.append(copy)
 
-    gather = {(w, s, k): z_copy(w, s, k) for w in (0, 1) for s in (1, 2, 3, 4) for k in (0, 1)}
+    gather = {
+        (w, s, k): z_copy(w, s, k)
+        for w in (0, 1) for s in (1, 2, 3, 4) for k in (0, 1) if s < 4 or w == k
+    }
     for kind in (0, 1):
         for way in (0, 1):
             start(gather[way, 1, kind])
@@ -93,11 +102,6 @@
     do_copies = [y_copy(do_ref, do_all.at[4 - t], 1, t) for t in (1, 3, 2)]
     for copy in q_copies + do_copies:
         start(copy)
-
-    k_a[0] = k_ref[...]
-    v_a[0] = v_ref[...]
-    q_all[0] = q_ref[...]
-    do_all[0] = do_ref[...]
 
     @pl.loop(0, NY)
     def _(i):
@@ -231,6 +235,8 @@
         for way in (0, 1):
             gather[way, 1, kind].wait_recv()
             start(gather[way, 2, kind])
+    for copy in own:
+        copy.wait()
     for copy in q_copies:
         copy.wait_recv()
     forward_near()
@@ -292,7 +298,10 @@
             device_id_type=MESH,
         )
 
-    scatter = {(w, s, k): r_copy(w, s, k) for w in (0, 1) for s in range(4) for k in (0, 1)}
+    scatter = {
+        (w, s, k): r_copy(w, s, k)
+        for w in (0, 1) for s in range(4) for k in (0, 1) if s > 0 or w == k
+    }
 
     def pass_on(step, way, kind):
         r = (4 - step) if way == 0 else (step - 4) % NZ
@@ -358,17 +367,31 @@
         copy.wait_send()
 
 
+def hand_over(*refs):
+    srcs, dsts, (buf, in_sem, out_sem) = refs[:4], refs[4:8], refs[8:]
+    loads = [pltpu.make_async_copy(src, buf.at[i], in_sem.at[i]) for i, src in enumerate(srcs)]
+    stores = [pltpu.make_async_copy(buf.at[i], dst, out_sem.at[i]) for i, dst in enumerate(dsts)]
+    for load in loads:
+        load.start()
+    for load, store in zip(loads, stores):
+        load.wait()
+        store.start()
+    for store in stores:
+        store.wait()
+
+
 def per_device(queries, keys, values, out_grad, radial_pick):
     width = queries.shape[1]
     heads = width // HD
     bf, f32 = jnp.bfloat16, jnp.float32
     vmem = pl.BlockSpec(memory_space=pltpu.VMEM)
+    hbm = pl.BlockSpec(memory_space=pl.ANY)
     shape = jax.ShapeDtypeStruct((FT, width), bf)
     dma = pltpu.SemaphoreType.DMA
-    return pl.pallas_call(
+    outs = pl.pallas_call(
         kernel,
         out_shape=(shape,) * 4,
-        in_specs=[pl.BlockSpec(memory_space=pltpu.SMEM)] + [vmem] * 4,
+        in_specs=[pl.BlockSpec(memory_space=pltpu.SMEM)] + [hbm] * 4,
         out_specs=(vmem,) * 4,
         scratch_shapes=[
             pltpu.VMEM((NY, FT, width), bf),
@@ -402,12 +425,22 @@
             dma((5, 3)),
             dma((2, 4, 2)),
             dma((2, 4, 2)),
+            dma((4,)),
         ],
         compiler_params=pltpu.CompilerParams(
             collective_id=0, has_side_effects=True, vmem_limit_bytes=60 * 1024 * 1024
         ),
         name="radial_attention",
     )(radial_pick, queries, keys, values, out_grad)
+    return pl.pallas_call(
+        hand_over,
+        out_shape=(shape,) * 4,
+        in_specs=[hbm] * 4,
+        out_specs=(hbm,) * 4,
+        scratch_shapes=[pltpu.VMEM((4, FT, width), bf), dma((4,)), dma((4,))],
+        compiler_params=pltpu.CompilerParams(vmem_limit_bytes=60 * 1024 * 1024),
+        name="hand_over",
+    )(*outs)
 
 
 def solution(mesh):

time: 86.9 us -> 84.5 us (0.972)
  local copies, waits for them, and re-layouts: 4.34 us -> 0 us
  Pallas kernels: 80.7 us -> 82.6 us
    unnamed x10 -> x0, local copies, waits for them, and re-layouts: 4.34 us -> none
    pallas_call x0 -> x1, Pallas kernels: none -> 1.96 us  [per_device(): pl.pallas_call(hand_over, out_shape=(shape,) * 4, in_specs=[hbm] * 4, out...]
where the time goes in v2:
time: 84.5 us; the launch traced here: 83.3 us
  Pallas kernels  82.6 us (98%)
    pallas_call x1, Pallas kernels, per_device(): pl.pallas_call(kernel, out_shape=(shape,) * 4, in_specs=[pl.BlockSpec(mem...  80.7 us
    pallas_call x1, Pallas kernels, per_device(): pl.pallas_call(hand_over, out_shape=(shape,) * 4, in_specs=[hbm] * 4, out...  1.96 us

profile of v2, /device:TPU:36, one launch (start us, length us, event | category | flops | bytes accessed | tf_op | source)
XLA Modules:
  0.0 83.3 jit_solution(7421204715058167115)
XLA Ops:
  0.6 80.7 %radial_attention.1 = (bf16[256,384]{1,0:T(8,128)(2,1)}, bf16[256,384]{1,0:T(8,128)(2,1)}, bf16[256,384]{1,0:T(8,128)(2,1)}, bf16[256,384]{1,0:T(8,128)(2,1)}) custom-call(s32[32,32]{1,0:T(8,128)} %pick_ref.1, bf16[256,384]{1,0:T(8,128)(2,1)} %q_ref.1, bf16[256,384]{1,0:T(8,128)(2,1)} %k_ref.1, bf16[256,384]{1,0:T(8,128)(2,1)} %v_ref.1, bf16[256,384]{1,0:T(8,128)(2,1)} %do_ref.1), custom_call_target="tpu_custom_call" | custom-call | tf_op jit(solution)/shard_map/radial_attention/pallas_call | solution.py:391
  81.3 2.0 %hand_over.1 = (bf16[256,384]{1,0:T(8,128)(2,1)}, bf16[256,384]{1,0:T(8,128)(2,1)}, bf16[256,384]{1,0:T(8,128)(2,1)}, bf16[256,384]{1,0:T(8,128)(2,1)}) custom-call(bf16[256,384]{1,0:T(8,128)(2,1)} %get-tuple-element.8.refs_0_, bf16[256,384]{1,0:T(8,128)(2,1)} %get-tuple-element.9.refs_1_, bf16[256,384]{1,0:T(8,128)(2,1)} %get-tuple-element.10.refs_2_, ...), custom_call_target="tpu_custom_call" | custom-call | tf_op jit(solution)/shard_map/hand_over/pallas_call | solution.py:435

commit v3 on v2

v3 whole, which is shorter than its diff:
```python
import functools

import jax
import jax.numpy as jnp
from jax import lax
from jax.experimental import pallas as pl
from jax.experimental.pallas import tpu as pltpu
from jax.sharding import PartitionSpec as P

HD = 128
BLOCK = 64
NZ = 8
NY = 4
FT = 256
NEG = -1e30
FLOOR = -1e20
MESH = pl.DeviceIdType.MESH

NEAR, FAR0, FAR1, FAR2, FAR3, KEYS = 0, 256, 448, 576, 704, 768

NT = (((1,), (1,)), ((), ()))
NN = (((1,), (0,)), ((), ()))
TN = (((0,), (0,)), ((), ()))


def mm(a, b, dims):
    return lax.dot_general(a, b, dims, preferred_element_type=jnp.float32)


def kernel(
    pick_ref, q_ref, k_ref, v_ref, do_ref,
    out_ref, dq_ref, dk_ref, dv_ref,
    q_all, do_all, do_t, k_a, v_a, k_b, v_b, k_c, v_c, k_d, v_d,
    k_sel, v_sel, sc, run, st, dl, fin, o_t, dq_t, o_send, o_recv, dq_send, dq_recv, acc,
    rs_send, rs_recv,
    z_ssem, z_rsem, y_ssem, y_rsem, r_ssem, r_rsem, l_sem,
):
    width = q_ref.shape[1]
    heads = width // HD
    scale = HD ** -0.5
    half = FT // 2
    me = lax.axis_index("ctx")
    z, y = me // NY, me % NY

    def at(dz, dy):
        return {"ctx": ((z + dz + NZ) % NZ) * NY + (y + dy) % NY}

    def cols(h):
        return slice(h * HD, (h + 1) * HD)

    own = [
        pltpu.make_async_copy(src, dst.at[0], l_sem.at[i])
        for i, (src, dst) in enumerate(((k_ref, k_a), (v_ref, v_a), (q_ref, q_all), (do_ref, do_all)))
    ]
    for copy in own:
        copy.start()
    barrier = pltpu.get_barrier_semaphore()
    for peer in (at(1, 0), at(-1, 0), at(0, 1), at(0, 2), at(0, 3)):
        pl.semaphore_signal(barrier, inc=1, device_id=peer, device_id_type=MESH)
    pl.semaphore_wait(barrier, 5)

    places = {0: 0, 1: 1, -1: 2, 2: 0, -2: 1, 3: 0, -3: 1, 4: 0, -4: 0}
    stores = {0: (k_a, v_a), 1: (k_a, v_a), 2: (k_b, v_b), 3: (k_c, v_c), 4: (k_d, v_d)}

    def z_copy(way, step, kind, part):
        sign = -1 if way == 0 else 1
        rows = slice(0, FT) if part is None else slice(part * half, (part + 1) * half)
        if step == 1:
            src = (k_ref, v_ref)[kind].at[rows]
        else:
            src = stores[step - 1][kind].at[places[sign * (step - 1)], rows]
        return pltpu.make_async_remote_copy(
            src_ref=src,
            dst_ref=stores[step][kind].at[places[sign * step], rows],
            send_sem=z_ssem.at[way, step - 1, kind, part or 0],
            recv_sem=z_rsem.at[way, step - 1, kind, part or 0],
            device_id=at(-sign, 0),
            device_id_type=MESH,
        )

    def y_copy(src, dst, what, t):
        return pltpu.make_async_remote_copy(
            src_ref=src,
            dst_ref=dst,
            send_sem=y_ssem.at[what, t - 1],
            recv_sem=y_rsem.at[what, 3 - t],
            device_id=at(0, t),
            device_id_type=MESH,
        )

    sent = []

    def start(copy):
        copy.start()
        sent.append(copy)

    gather = {}

    def put(step, kind, part=None):
        for way in (0, 1):
            piece = None if part is None else way ^ part
            gather[way, step, kind, part] = z_copy(way, step, kind, piece)
            start(gather[way, step, kind, part])

    def got(step, kind, part=None):
        for way in (0, 1):
            gather[way, step, kind, part].wait_recv()

    put(1, 0)
    put(1, 1)
    q_copies = {t: y_copy(q_ref, q_all.at[4 - t], 0, t) for t in (1, 3, 2)}
    do_copies = {t: y_copy(do_ref, do_all.at[4 - t], 1, t) for t in (1, 3, 2)}
    for copy in list(q_copies.values()) + list(do_copies.values()):
        start(copy)

    @pl.loop(0, NY)
    def _(i):
        for j in (0, 1):
            run[j, i, 0:heads] = jnp.full((heads, FT), FLOOR, jnp.float32)
            run[j, i, heads : 2 * heads] = jnp.zeros((heads, FT), jnp.float32)
        o_t[i] = jnp.zeros((width, FT), jnp.float32)
        dq_t[i] = jnp.zeros((width, FT), jnp.float32)

    @pl.loop(0, NZ)
    def _(i):
        for kind in (0, 1):
            acc[i, kind] = jnp.zeros((FT, width), jnp.float32)

    tile = lax.broadcasted_iota(jnp.int32, (1, FT), 1) // BLOCK

    group0 = ((0, k_a, v_a, 0), (1, k_a, v_a, 1), (-1, k_a, v_a, 2))
    group1 = ((2, k_b, v_b, 0), (-2, k_b, v_b, 1))
    group2 = ((3, k_c, v_c, 0), (-3, k_c, v_c, 1))
    group3 = ((4, k_d, v_d, 0),)

    def chosen(qi, r):
        a = z * NY + (y + qi) % NY
        b = ((z + r + NZ) % NZ) * NY + y
        return pick_ref[a, b], jnp.abs(a - b)

    def bias_row(qi, r):
        pick, dist = chosen(qi, r)
        want = jnp.broadcast_to(pick, (1, FT)) >> 2
        row = jnp.where(tile == want, 0.0, NEG).astype(jnp.float32)
        row = jnp.maximum(row, jnp.where(dist < 4, 0.0, NEG).astype(jnp.float32))
        return jnp.minimum(row, jnp.where(dist < 2, NEG, 0.0).astype(jnp.float32))

    def select(group, begin, kinds):
        begin -= FAR0

        @pl.loop(0, NY)
        def _(qi):
            for g, (r, k, v, i) in enumerate(group):
                pick, _ = chosen(qi, r)
                place = jnp.broadcast_to(pick, (1, width)) & 3
                hits = [jnp.where(place == n, 1.0, 0.0).astype(k.dtype) for n in range(4)]
                to = slice(begin + g * BLOCK, begin + (g + 1) * BLOCK)
                for kind in kinds:
                    ref, dst = ((k, k_sel), (v, v_sel))[kind]
                    parts = [ref[i, n * BLOCK : (n + 1) * BLOCK] * hits[n] for n in range(4)]
                    dst[qi, to] = (parts[0] + parts[1]) + (parts[2] + parts[3])

    def rows(parts):
        return parts[0] if len(parts) == 1 else jnp.concatenate(parts, 0)

    def merge(j, qi, h, s):
        m_old = run[j, qi, h : h + 1]
        l_old = run[j, qi, heads + h : heads + h + 1]
        m_new = jnp.maximum(m_old, jnp.max(s, axis=0, keepdims=True))
        p = jnp.exp(s - m_new)
        alpha = jnp.exp(m_old - m_new)
        run[j, qi, h : h + 1] = m_new
        run[j, qi, heads + h : heads + h + 1] = l_old * alpha + jnp.sum(p, axis=0, keepdims=True)
        return p, alpha

    def update(qi, h, s, values):
        p, alpha = merge(0, qi, h, s)
        o_t[qi, cols(h)] = o_t[qi, cols(h)] * alpha + mm(values, p.astype(jnp.bfloat16), TN)

    def forward_far(group, begin, whole):
        size = BLOCK * len(group)
        select(group, begin, (0, 1) if whole else (0,))

        @pl.loop(0, NY)
        def _(qi):
            bias = [bias_row(qi, r) for r, _, _, _ in group]
            bias = rows([jnp.broadcast_to(row, (BLOCK, FT)) for row in bias])
            for h in range(heads):
                ks = k_sel[qi, begin - FAR0 : begin - FAR0 + size, cols(h)]
                s = mm(ks, q_all[qi, :, cols(h)], NT) * scale + bias
                sc[qi, h, begin : begin + size] = s
                if whole:
                    update(qi, h, s, v_sel[qi, begin - FAR0 : begin - FAR0 + size, cols(h)])
                else:
                    merge(1, qi, h, s)

    def near_place(i):
        qi = jnp.where(i == 2, 3, i)
        over = ((i == 1) & (y == NY - 1)) | ((i == 2) & (y == 0))
        slot = jnp.where(over, jnp.where(i == 1, 2, 1), 0)
        r = jnp.where(over, jnp.where(i == 1, NZ - 1, 1), 0)
        dead = ((i == 1) & (y == NY - 1) & (z == 0)) | ((i == 2) & (y == 0) & (z == NZ - 1))
        return qi, slot, r, jnp.where(dead, NEG, 0.0).astype(jnp.float32)

    def forward_near():
        @pl.loop(0, 3)
        def _(i):
            qi, slot, _, bias = near_place(i)
            for h in range(heads):
                s = mm(k_a[slot, :, cols(h)], q_all[qi, :, cols(h)], NT) * scale + bias
                sc[qi, h, NEAR : NEAR + FT] = s
                update(qi, h, s, v_a[slot, :, cols(h)])

    def scatter_add(group, qi, h, kind, value):
        for g, (r, _, _, _) in enumerate(group):
            pick, _ = chosen(qi, r)
            place = jnp.broadcast_to(pick, (1, HD)) & 3
            part = value[g * BLOCK : (g + 1) * BLOCK]
            for n in range(FT // BLOCK):
                hit = jnp.where(place == n, 1.0, 0.0).astype(jnp.float32)
                acc[r % NZ, kind, n * BLOCK : (n + 1) * BLOCK, cols(h)] += part * hit

    def value_part(qi, h, p):
        return mm(p.astype(jnp.bfloat16), do_all[qi, :, cols(h)], NN)

    def key_part(qi, h, p, ks, vs):
        dp = mm(vs, do_all[qi, :, cols(h)], NT)
        ds = (p * (dp - fin[qi, heads + h : heads + h + 1])).astype(jnp.bfloat16)
        dq_t[qi, cols(h)] = dq_t[qi, cols(h)] + mm(ks, ds, TN)
        return mm(ds, q_all[qi, :, cols(h)], NN) * scale

    def backward_far(group, begin, kinds):
        size = BLOCK * len(group)

        @pl.loop(0, NY)
        def _(qi):
            for h in range(heads):
                p = sc[qi, h, begin : begin + size]
                if 1 in kinds:
                    p = jnp.exp(p - fin[qi, h : h + 1])
                    if 0 not in kinds:
                        sc[qi, h, begin : begin + size] = p
                    scatter_add(group, qi, h, 1, value_part(qi, h, p))
                if 0 in kinds:
                    ks = k_sel[qi, begin - FAR0 : begin - FAR0 + size, cols(h)]
                    vs = v_sel[qi, begin - FAR0 : begin - FAR0 + size, cols(h)]
                    scatter_add(group, qi, h, 0, key_part(qi, h, p, ks, vs))

    def backward_near():
        @pl.loop(0, 3)
        def _(i):
            qi, slot, r, _ = near_place(i)
            for h in range(heads):
                p = jnp.exp(sc[qi, h, NEAR : NEAR + FT] - fin[qi, h : h + 1])
                acc[r, 1, :, cols(h)] += value_part(qi, h, p)
                ks, vs = k_a[slot, :, cols(h)], v_a[slot, :, cols(h)]
                acc[r, 0, :, cols(h)] += key_part(qi, h, p, ks, vs)

    got(1, 0)
    put(2, 0)
    got(1, 1)
    put(2, 1, 0)
    for copy in own:
        copy.wait()
    q_copies[1].wait_recv()
    q_copies[3].wait_recv()
    forward_near()
    got(2, 0)
    put(3, 0)
    put(2, 1, 1)
    q_copies[2].wait_recv()
    forward_far(group0, FAR0, True)
    got(3, 0)
    put(4, 0, 0)
    got(2, 1, 0)
    put(3, 1, 0)
    forward_far(group2, FAR2, False)
    got(2, 1, 1)
    put(3, 1, 1)
    forward_far(group1, FAR1, True)
    got(4, 0, 0)
    forward_far(group3, FAR3, False)

    for qi in range(NY):
        m = [run[j, qi, 0:heads] for j in (0, 1)]
        l = [run[j, qi, heads : 2 * heads] for j in (0, 1)]
        top = jnp.maximum(m[0], m[1])
        st[0, qi, 0:heads] = top
        st[0, qi, heads : 2 * heads] = l[0] * jnp.exp(m[0] - top) + l[1] * jnp.exp(m[1] - top)
    st_copies = [y_copy(st.at[0], st.at[4 - t], 2, t) for t in (2, 1, 3)]
    for copy in st_copies:
        start(copy)
    got(3, 1, 0)
    put(4, 1, 0)
    for copy in do_copies.values():
        copy.wait_recv()

    @pl.loop(0, NY)
    def _(i):
        for h in range(heads):
            do_t[i, cols(h)] = do_all[i, :, cols(h)].astype(jnp.float32).T

    for copy in st_copies:
        copy.wait_recv()
    for qi in range(NY):
        peer = [st[s, (qi - s) % NY] for s in range(NY)]
        top = functools.reduce(jnp.maximum, [x[0:heads] for x in peer])
        total = functools.reduce(
            jnp.add, [x[heads : 2 * heads] * jnp.exp(x[0:heads] - top) for x in peer]
        )
        fin[qi, 0:heads] = top + jnp.log(total)

    scatter = {}

    def pass_on(step, kind, part):
        for way in (0, 1):
            r = (4 - step) if way == 0 else (step - 4) % NZ
            piece = way ^ part
            where = slice(piece * half, (piece + 1) * half)
            value = acc[r, kind, where]
            if step >= 2 or (step == 1 and part == 0):
                scatter[way, step - 1, kind, part].wait_recv()
                value = value + rs_recv[way, step - 1, kind, where].astype(jnp.float32)
            rs_send[way, step, kind, where] = value.astype(jnp.bfloat16)
            copy = pltpu.make_async_remote_copy(
                src_ref=rs_send.at[way, step, kind, where],
                dst_ref=rs_recv.at[way, step, kind, where],
                send_sem=r_ssem.at[way, step, kind, part],
                recv_sem=r_rsem.at[way, step, kind, part],
                device_id=at(1 if way == 0 else -1, 0),
                device_id_type=MESH,
            )
            scatter[way, step, kind, part] = copy
            start(copy)

    backward_far(group3, FAR3, (1,))
    pass_on(0, 1, 0)
    backward_far(group2, FAR2, (1,))
    pass_on(1, 1, 1)
    got(3, 1, 1)
    got(4, 1, 0)
    select(group2, FAR2, (1,))
    select(group3, FAR3, (1,))

    @pl.loop(0, NY)
    def _(qi):
        for h in range(heads):
            p = sc[qi, h, FAR2:KEYS].astype(jnp.bfloat16)
            vs = v_sel[qi, FAR2 - FAR0 : KEYS - FAR0, cols(h)]
            keep = jnp.exp(run[0, qi, h : h + 1] - fin[qi, h : h + 1])
            o = o_t[qi, cols(h)] * keep + mm(vs, p, TN)
            o_t[qi, cols(h)] = o
            dl[0, qi, h : h + 1] = jnp.sum(o * do_t[qi, cols(h)], axis=0, keepdims=True)

    dl_copies = [y_copy(dl.at[0], dl.at[4 - t], 5, t) for t in (2, 1, 3)]
    for copy in dl_copies:
        start(copy)
    pass_on(1, 1, 0)
    o_copies = []
    for t in (2, 1, 3):
        o_send[t - 1] = o_t[t].astype(jnp.bfloat16)
        o_copies.append(y_copy(o_send.at[t - 1], o_recv.at[3 - t], 3, t))
        start(o_copies[-1])
    backward_far(group1, FAR1, (1,))
    pass_on(2, 1, 1)
    for copy in dl_copies:
        copy.wait_recv()
    for qi in range(NY):
        fin[qi, heads : 2 * heads] = functools.reduce(
            jnp.add, [dl[s, (qi - s) % NY] for s in range(NY)]
        )
    pass_on(2, 1, 0)
    backward_far(group3, FAR3, (0,))
    pass_on(0, 0, 0)
    backward_far(group2, FAR2, (0,))
    pass_on(1, 0, 1)
    backward_far(group1, FAR1, (0,))
    pass_on(1, 0, 0)
    backward_far(group0, FAR0, (0, 1))
    dq_copies = []

    def send_dq(t):
        dq_send[t - 1] = (dq_t[t] * scale).astype(jnp.bfloat16)
        dq_copies.append(y_copy(dq_send.at[t - 1], dq_recv.at[3 - t], 4, t))
        start(dq_copies[-1])

    send_dq(2)
    pass_on(2, 0, 1)
    backward_near()
    send_dq(1)
    send_dq(3)
    pass_on(3, 1, 1)
    pass_on(2, 0, 0)
    pass_on(3, 1, 0)
    pass_on(3, 0, 1)
    pass_on(3, 0, 0)

    for copy in o_copies:
        copy.wait_recv()
    for h in range(heads):
        total = o_t[0, cols(h)]
        for i in range(3):
            total = total + o_recv[i, cols(h)].astype(jnp.float32)
        out_ref[:, cols(h)] = total.T.astype(jnp.bfloat16)
    for copy in dq_copies:
        copy.wait_recv()
    for h in range(heads):
        total = dq_t[0, cols(h)] * scale
        for i in range(3):
            total = total + dq_recv[i, cols(h)].astype(jnp.float32)
        dq_ref[:, cols(h)] = total.T.astype(jnp.bfloat16)
    for kind, ref in ((1, dv_ref), (0, dk_ref)):
        for way in (0, 1):
            for part in (0, 1):
                scatter[way, 3, kind, part].wait_recv()
        total = acc[0, kind]
        for way in (0, 1):
            total = total + rs_recv[way, 3, kind].astype(jnp.float32)
        ref[...] = total.astype(jnp.bfloat16)
    for copy in sent:
        copy.wait_send()


def hand_over(*refs):
    srcs, dsts, (buf, in_sem, out_sem) = refs[:4], refs[4:8], refs[8:]
    loads = [pltpu.make_async_copy(src, buf.at[i], in_sem.at[i]) for i, src in enumerate(srcs)]
    stores = [pltpu.make_async_copy(buf.at[i], dst, out_sem.at[i]) for i, dst in enumerate(dsts)]
    for load in loads:
        load.start()
    for load, store in zip(loads, stores):
        load.wait()
        store.start()
    for store in stores:
        store.wait()


def per_device(queries, keys, values, out_grad, radial_pick):
    width = queries.shape[1]
    heads = width // HD
    bf, f32 = jnp.bfloat16, jnp.float32
    vmem = pl.BlockSpec(memory_space=pltpu.VMEM)
    hbm = pl.BlockSpec(memory_space=pl.ANY)
    shape = jax.ShapeDtypeStruct((FT, width), bf)
    dma = pltpu.SemaphoreType.DMA
    outs = pl.pallas_call(
        kernel,
        out_shape=(shape,) * 4,
        in_specs=[pl.BlockSpec(memory_space=pltpu.SMEM)] + [hbm] * 4,
        out_specs=(vmem,) * 4,
        scratch_shapes=[
            pltpu.VMEM((NY, FT, width), bf),
            pltpu.VMEM((NY, FT, width), bf),
            pltpu.VMEM((NY, width, FT), f32),
            pltpu.VMEM((3, FT, width), bf),
            pltpu.VMEM((3, FT, width), bf),
            pltpu.VMEM((2, FT, width), bf),
            pltpu.VMEM((2, FT, width), bf),
            pltpu.VMEM((2, FT, width), bf),
            pltpu.VMEM((2, FT, width), bf),
            pltpu.VMEM((1, FT, width), bf),
            pltpu.VMEM((1, FT, width), bf),
            pltpu.VMEM((NY, KEYS - FAR0, width), bf),
            pltpu.VMEM((NY, KEYS - FAR0, width), bf),
            pltpu.VMEM((NY, heads, KEYS, FT), f32),
            pltpu.VMEM((2, NY, 2 * heads, FT), f32),
            pltpu.VMEM((NY, NY, 2 * heads, FT), f32),
            pltpu.VMEM((NY, NY, heads, FT), f32),
            pltpu.VMEM((NY, 2 * heads, FT), f32),
            pltpu.VMEM((NY, width, FT), f32),
            pltpu.VMEM((NY, width, FT), f32),
            pltpu.VMEM((3, width, FT), bf),
            pltpu.VMEM((3, width, FT), bf),
            pltpu.VMEM((3, width, FT), bf),
            pltpu.VMEM((3, width, FT), bf),
            pltpu.VMEM((NZ, 2, FT, width), f32),
            pltpu.VMEM((2, 4, 2, FT, width), bf),
            pltpu.VMEM((2, 4, 2, FT, width), bf),
            dma((2, 4, 2, 2)),
            dma((2, 4, 2, 2)),
            dma((6, 3)),
            dma((6, 3)),
            dma((2, 4, 2, 2)),
            dma((2, 4, 2, 2)),
            dma((4,)),
        ],
        compiler_params=pltpu.CompilerParams(
            collective_id=0, has_side_effects=True, vmem_limit_bytes=60 * 1024 * 1024
        ),
        name="radial_attention",
    )(radial_pick, queries, keys, values, out_grad)
    return pl.pallas_call(
        hand_over,
        out_shape=(shape,) * 4,
        in_specs=[hbm] * 4,
        out_specs=(hbm,) * 4,
        scratch_shapes=[pltpu.VMEM((4, FT, width), bf), dma((4,)), dma((4,))],
        compiler_params=pltpu.CompilerParams(vmem_limit_bytes=60 * 1024 * 1024),
        name="hand_over",
    )(*outs)


def solution(mesh):
    spec = P(("dp", "ctx"), "head")
    return jax.shard_map(
        per_device,
        mesh=mesh,
        in_specs=(spec, spec, spec, spec, P()),
        out_specs=(spec,) * 4,
        check_vma=False,
    )
```

time: 84.5 us -> 80.5 us (0.953)
  Pallas kernels: 82.6 us -> 79.2 us
    pallas_call x1, Pallas kernels: 80.7 us -> 77.2 us  [per_device(): pl.pallas_call(kernel, out_shape=(shape,) * 4, in_specs=[pl.BlockSpec(mem...]
where the time goes in v3:
time: 80.5 us; the launch traced here: 79.8 us
  Pallas kernels  79.2 us (98%)
    pallas_call x1, Pallas kernels, per_device(): pl.pallas_call(kernel, out_shape=(shape,) * 4, in_specs=[pl.BlockSpec(mem...  77.2 us
    pallas_call x1, Pallas kernels, per_device(): pl.pallas_call(hand_over, out_shape=(shape,) * 4, in_specs=[hbm] * 4, out...  1.96 us

profile of v3, /device:TPU:36, one launch (start us, length us, event | category | flops | bytes accessed | tf_op | source)
XLA Modules:
  0.0 79.8 jit_solution(7155811856066061761)
XLA Ops:
  0.6 77.2 %radial_attention.1 = (bf16[256,384]{1,0:T(8,128)(2,1)}, bf16[256,384]{1,0:T(8,128)(2,1)}, bf16[256,384]{1,0:T(8,128)(2,1)}, bf16[256,384]{1,0:T(8,128)(2,1)}) custom-call(s32[32,32]{1,0:T(8,128)} %pick_ref.1, bf16[256,384]{1,0:T(8,128)(2,1)} %q_ref.1, bf16[256,384]{1,0:T(8,128)(2,1)} %k_ref.1, bf16[256,384]{1,0:T(8,128)(2,1)} %v_ref.1, bf16[256,384]{1,0:T(8,128)(2,1)} %do_ref.1), custom_call_target="tpu_custom_call" | custom-call | tf_op jit(solution)/shard_map/radial_attention/pallas_call | solution.py:445
  77.9 2.0 %hand_over.1 = (bf16[256,384]{1,0:T(8,128)(2,1)}, bf16[256,384]{1,0:T(8,128)(2,1)}, bf16[256,384]{1,0:T(8,128)(2,1)}, bf16[256,384]{1,0:T(8,128)(2,1)}) custom-call(bf16[256,384]{1,0:T(8,128)(2,1)} %get-tuple-element.8.refs_0_, bf16[256,384]{1,0:T(8,128)(2,1)} %get-tuple-element.9.refs_1_, bf16[256,384]{1,0:T(8,128)(2,1)} %get-tuple-element.10.refs_2_, ...), custom_call_target="tpu_custom_call" | custom-call | tf_op jit(solution)/shard_map/hand_over/pallas_call | solution.py:491
